TPU v7x, 32 devices: a whole 2x2x4 slice. The times are simulated.
32 devices in a mesh: parts: 1, head: 32 (over z, y, x, core).
Axes of the slice: x: 2, y: 2, z: 4, core: 2. Of those that a mesh axis runs over, the one named last changes fastest.
Arguments:
- queries: bfloat16 [8, 2048, 2048], P('parts', 'head'), may hold values from -6 to 6
- keys: bfloat16 [8, 2048, 2048], P('parts', 'head'), may hold values from -6 to 6
- values: bfloat16 [8, 2048, 2048], P('parts', 'head'), may hold values from -6 to 6
- slot_positions: int32 [8, 2048], P('parts', 'head'), may hold values from 0 to 2047, each once within a row
- counts: int32 [8], P('parts'), may hold values from 16 to 2048, as said below
- timesteps: int32 [8], P('parts'), may hold values from 0 to 999
- labels: int32 [8], P('parts'), may hold values from 0 to 127
- time_weight: bfloat16 [256, 4096], replicated, may hold values from -0.375 to 0.375
- norm_gain: float32 [2048], replicated, may hold values from 0.25 to 1.75
- gate_weight: bfloat16 [2048, 8192], P(None, 'head'), may hold values from -0.125 to 0.125
- up_weight: bfloat16 [2048, 8192], P(None, 'head'), may hold values from -0.125 to 0.125
- down_weight: bfloat16 [8192, 2048], P('head'), may hold values from -0.0625 to 0.0625
- class_weight: bfloat16 [2048, 128], replicated, may hold values from -3 to 3
- class_bias: float32 [128], replicated, may hold values from -5 to 112
Outputs:
- attention: bfloat16 [256, 2048, 64], P(('parts', 'head'))
- guidance: float32 [8, 128, 2048], P('parts', 'head')
Inputs may be any that keep to these rules, and one draw needn't show every extreme that they name: `counts`: multiples of 16; in every part one shower has exactly 2048. `slot_positions`: each shower's row is a permutation of 0 to 2047.
All inputs are finite; a program needn't handle non-finite values.
Results may differ from a plain program's by a relative error of at most 0.01.
The roundings to bfloat16 on the way count: a program that leaves them out, or rounds other values in their place, can miss the bound.
Values may be sent and summed in bfloat16 or wider, within the bound.
A program may use at most 192 MiB of HBM per device.

v0:
```python
import math
import jax
import jax.numpy as jnp
from jax import lax
from jax.sharding import PartitionSpec as P

HEADS = 32
POOL = 16
epsilon = 1e-06


def sinusoid(steps, embed_width):
    half_width = embed_width // 2
    frequency = jnp.exp(-math.log(10000.0) * jnp.arange(half_width, dtype=jnp.float32) / half_width)
    angles = steps.astype(jnp.float32)[:, None] * frequency[None, :]
    return jnp.concatenate([jnp.cos(angles), jnp.sin(angles)], axis=1)


def attend_pair(pair_data):
    query_rows, key_rows, value_rows, key_valid = pair_data
    head_dim = query_rows.shape[1]
    scores = jnp.dot(query_rows, key_rows.T, preferred_element_type=jnp.float32) * head_dim ** (
        -0.5
    )
    scores = jnp.where(key_valid[None, :], scores, -jnp.inf)
    peak = jnp.max(scores, axis=1, keepdims=True)
    exponent = jnp.exp(scores - peak)
    weights = (exponent / jnp.sum(exponent, axis=1, keepdims=True)).astype(jnp.bfloat16)
    mixed = jnp.dot(weights, value_rows, preferred_element_type=jnp.float32)
    return (mixed * key_valid[:, None].astype(jnp.float32)).astype(jnp.bfloat16)


def body(
    queries,
    keys,
    values,
    slot_positions,
    counts,
    timesteps,
    labels,
    time_weight,
    norm_gain,
    gate_weight,
    up_weight,
    down_weight,
    class_weight,
    class_bias,
):
    devices = lax.axis_size("head")
    device_index = lax.axis_index("head")
    showers, local_length, model_width = queries.shape
    head_dim = model_width // HEADS
    pairs_here = showers * HEADS // devices
    windows = local_length * devices // POOL
    per_device = windows // devices
    row_total = showers * windows

    def to_pairs(block):
        return (
            block.reshape(showers, local_length, HEADS, head_dim)
            .transpose(0, 2, 1, 3)
            .reshape(devices, pairs_here, local_length, head_dim)
        )

    valid_slots = slot_positions < counts[:, None]
    slot_flags = jnp.broadcast_to(
        valid_slots.astype(jnp.bfloat16)[:, None, :], (showers, HEADS, local_length)
    ).reshape(devices, pairs_here, local_length)
    query_rows = lax.all_to_all(to_pairs(queries), "head", split_axis=0, concat_axis=2, tiled=True)
    key_rows = lax.all_to_all(to_pairs(keys), "head", split_axis=0, concat_axis=2, tiled=True)
    value_rows = lax.all_to_all(to_pairs(values), "head", split_axis=0, concat_axis=2, tiled=True)
    flag_rows = lax.all_to_all(slot_flags, "head", split_axis=0, concat_axis=2, tiled=True)
    pair_count = query_rows.shape[1]
    flag_rows = flag_rows[0]
    attention_part = lax.map(
        attend_pair, (query_rows[0], key_rows[0], value_rows[0], flag_rows > 0.5)
    )
    flag_values = flag_rows.astype(jnp.float32)
    window_count = jnp.sum(flag_values.reshape(pair_count, windows, POOL), axis=2)
    window_sum = jnp.sum(
        attention_part.astype(jnp.float32).reshape(pair_count, windows, POOL, head_dim), axis=2
    )
    pooled_part = (window_sum / jnp.maximum(window_count, 1.0)[:, :, None]).astype(jnp.bfloat16)
    attention, pooled, window_count = (
        attention_part,
        pooled_part,
        window_count.astype(jnp.bfloat16),
    )
    pooled_all, count_all = (
        lax.all_gather(pooled, "head", axis=0, tiled=True),
        lax.all_gather(window_count, "head", axis=0, tiled=True),
    )
    pooled_rows = (
        pooled_all.reshape(showers, HEADS, devices, per_device, head_dim)
        .transpose(2, 0, 3, 1, 4)
        .reshape(devices, showers, per_device, model_width)
        .astype(jnp.float32)
    )
    row_count = (
        count_all.reshape(showers, HEADS, devices, per_device)[:, 0]
        .transpose(1, 0, 2)
        .astype(jnp.float32)
    )
    embedding = sinusoid(timesteps, time_weight.shape[0]).astype(jnp.bfloat16)
    modulation = jnp.dot(embedding, time_weight, preferred_element_type=jnp.float32)
    shifts = modulation[:, None, :model_width]
    scales = 1.0 + modulation[:, None, model_width:]
    inverse_rms = lax.rsqrt(jnp.mean(pooled_rows * pooled_rows, axis=3, keepdims=True) + epsilon)
    unit_rows = pooled_rows * inverse_rms
    normed = (
        (unit_rows * norm_gain * scales[None] + shifts[None])
        .astype(jnp.bfloat16)
        .reshape(row_total, model_width)
    )
    own_pooled = lax.dynamic_slice_in_dim(pooled_rows, device_index, 1, 0)[0]
    own_count = lax.dynamic_slice_in_dim(row_count, device_index, 1, 0)[0]
    own_units = lax.dynamic_slice_in_dim(unit_rows, device_index, 1, 0)[0]
    own_inverse = lax.dynamic_slice_in_dim(inverse_rms, device_index, 1, 0)[0]
    shower_counts = counts.astype(jnp.float32)
    class_matrix = class_weight.astype(jnp.float32)
    target = (
        labels[:, None] == jnp.arange(class_matrix.shape[1], dtype=jnp.int32)[None, :]
    ).astype(jnp.float32)
    gate_out = jnp.dot(normed, gate_weight, preferred_element_type=jnp.float32)
    up_out = jnp.dot(normed, up_weight, preferred_element_type=jnp.float32)
    activated = jax.nn.silu(gate_out)
    hidden = (activated * up_out).astype(jnp.bfloat16)
    own_mlp = lax.psum_scatter(
        jnp.dot(hidden, down_weight, preferred_element_type=jnp.float32),
        "head",
        scatter_dimension=0,
        tiled=True,
    ).reshape(showers, per_device, model_width)
    partial_value = jnp.sum(own_count[:, :, None] * (own_pooled + own_mlp), axis=1)
    features = lax.psum(partial_value, "head") / shower_counts[:, None]
    logits = jnp.dot(features, class_matrix, precision=lax.Precision.HIGHEST) + class_bias
    exponent = jnp.exp(logits - jnp.max(logits, axis=1, keepdims=True))
    probability = exponent / jnp.sum(exponent, axis=1, keepdims=True)
    feature_grad = jnp.dot(target - probability, class_matrix.T, precision=lax.Precision.HIGHEST)
    row_grads = (
        row_count[:, :, :, None]
        / shower_counts[None, :, None, None]
        * feature_grad[None, :, None, :]
    )
    hidden_grad = jnp.dot(
        row_grads.astype(jnp.bfloat16).reshape(row_total, model_width),
        down_weight.T,
        preferred_element_type=jnp.float32,
    )
    sigmoid_gate = jax.nn.sigmoid(gate_out)
    gate_grad = (
        hidden_grad * up_out * sigmoid_gate * (1.0 + gate_out * (1.0 - sigmoid_gate))
    ).astype(jnp.bfloat16)
    up_grad = (hidden_grad * activated).astype(jnp.bfloat16)
    normed_grad = lax.psum_scatter(
        jnp.dot(gate_grad, gate_weight.T, preferred_element_type=jnp.float32)
        + jnp.dot(up_grad, up_weight.T, preferred_element_type=jnp.float32),
        "head",
        scatter_dimension=0,
        tiled=True,
    ).reshape(showers, per_device, model_width)
    own_row_grads = lax.dynamic_slice_in_dim(row_grads, device_index, 1, 0)[0]
    unit_grad = normed_grad * norm_gain * scales
    pooled_grad = own_inverse * (
        unit_grad - own_units * jnp.mean(unit_grad * own_units, axis=2, keepdims=True)
    )
    guidance = windows * (own_row_grads + pooled_grad)
    return (attention, guidance)


def solution(mesh):
    in_specs = (
        P("parts", "head", None),
        P("parts", "head", None),
        P("parts", "head", None),
        P("parts", "head"),
        P("parts"),
        P("parts"),
        P("parts"),
        P(),
        P(),
        P(None, "head"),
        P(None, "head"),
        P("head", None),
        P(),
        P(),
    )
    out_specs = (P(("parts", "head"), None, None), P("parts", "head", None))
    return jax.shard_map(body, mesh=mesh, in_specs=in_specs, out_specs=out_specs, check_vma=False)
```

profile of v0, /device:TPU:0, one launch (start us, length us, event | category | flops | bytes accessed | tf_op | source)
XLA Modules:
  0.0 928.5 jit_solution(15136962674087946436)
XLA Ops:
  8.8 7.3 all-to-all-start
  29.0 7.9 reshape.178
  55.7 7.9 reshape.180
  63.6 28.0 %all-to-all-done.1 = bf16[32,2,16384]{2,1,0:T(2,128)(2,1)} async-done(((bf16[32,2,16384]{2,1,0:T(2,128)(2,1)}), bf16[32,2,16384]{2,1,0:T(2,128)(2,1)}, u32[]{:S(2)}, u32[]{:S(2)}) %all-to-all-start.1) | async-done | bytes 2097184 | tf_op jit(solution)/shard_map/all_to_all | solution.py:69
  108.8 7.9 reshape.182
  116.7 28.0 %all-to-all-done.2 = bf16[32,2,16384]{2,1,0:T(2,128)(2,1)} async-done(((bf16[32,2,16384]{2,1,0:T(2,128)(2,1)}), bf16[32,2,16384]{2,1,0:T(2,128)(2,1)}, u32[]{:S(2)}, u32[]{:S(2)}) %all-to-all-start.2) | async-done | bytes 2097184 | tf_op jit(solution)/shard_map/all_to_all | solution.py:70
  150.3 7.9 reshape.179
  163.8 7.9 reshape.181
  177.2 20.4 %all-to-all-done.3 = bf16[32,2,16384]{2,1,0:T(2,128)(2,1)} async-done(((bf16[32,2,16384]{2,1,0:T(2,128)(2,1)}), bf16[32,2,16384]{2,1,0:T(2,128)(2,1)}, u32[]{:S(2)}, u32[]{:S(2)}) %all-to-all-start.3) | async-done | bytes 2097184 | tf_op jit(solution)/shard_map/all_to_all | solution.py:71
  197.6 7.9 reshape.183
  211.1 119.2 %while.10 = (s32[]{:T(128)}, bf16[8,2048,64]{1,2,0:T(8,128)(2,1)}, pred[8,2048]{1,0:T(8,128)(4,1)S(1)}, bf16[8,2048,64]{2,1,0:T(8,128)(2,1)}, bf16[8,2048,64]{2,...) while((s32[]{:T(128)}, bf16[8,2048,64]{1,2,0:T(8,128)(2,1)}, pred[8,2048]{1,0:T(8,128)(4,1)S(1)}, ...), condition=%wide.region_3.4_spmd, body=%wide.region_0.3_spmd.sunk | while | flops 1124333568 | bytes 52238416 | solution.py:75
  348.5 10.4 %mul.175 = f32[1024,2048]{1,0:T(8,128)} reshape(f32[32,8,4,2048]{3,2,1,0:T(4,128)} %mul.174) | data formatting | bytes 16777216 | tf_op jit(solution)/shard_map/mul | solution.py:111
  364.2 10.0 %add.83 = f32[1024,2048]{1,0:T(8,128)} reshape(f32[32,8,4,2048]{3,2,1,0:T(4,128)} %add.82) | data formatting | bytes 16777216 | tf_op jit(solution)/shard_map/add | solution.py:111
  374.2 29.7 %all-gather.2.cloned.1.call-done = bf16[256,128,64]{1,2,0:T(8,128)(2,1)} async-done(((bf16[8,128,64]{1,2,0:T(8,128)(2,1)}), bf16[256,128,64]{1,2,0:T(8,128)(2,1)}) %all-gather.2.cloned.1.call-update) | async-done | bytes 4194320 | tf_op jit(solution)/shard_map/all_gather | solution.py:90
  409.5 12.7 %copy.135 = f32[256,128,64]{2,0,1:T(8,128)} copy(bf16[256,128,64]{1,2,0:T(8,128)(2,1)} %all-gather.2.cloned.1.call-done) | data formatting | bytes 12582912 | tf_op jit(solution)/shard_map/convert_element_type | solution.py:97
  422.2 11.9 %copy.137 = f32[32,8,4,32,64]{4,3,2,1,0:T(8,128)} copy(f32[32,8,4,32,64]{4,3,1,2,0:T(8,128)} %bitcast.115) | data formatting | bytes 16777216 | tf_op jit(solution)/shard_map/convert_element_type | solution.py:97
  434.0 14.8 %reshape.169 = f32[1024,2048]{1,0:T(8,128)} reshape(f32[32,8,4,32,64]{4,3,2,1,0:T(8,128)} %copy.137) | data formatting | bytes 16777216 | tf_op jit(solution)/shard_map/convert_element_type | solution.py:97
  448.9 10.4 %add_convert_fusion = bf16[1024,2048]{1,0:T(8,128)(2,1)S(1)} fusion(f32[1024,2048]{1,0:T(8,128)} %add.83, f32[1024,2048]{1,0:T(8,128)} %mul.175, f32[1024,2048]{1,0:T(8,128)} %reshape.169, f32[2048]{0:T(1024)S(1)} %copy-done.8, f32[1024]{0:T(1024)S(1)} %rsqrt.18), kind=kLoop, calls=%fused_computation.24 | loop fusion | flops 10485760 | bytes 29372416 | tf_op jit(solution)/shard_map/convert_element_type | solution.py:112
  467.4 39.9 %all_gather.6 = bf16[256,128]{1,0:T(8,128)(2,1)S(1)} all-gather(bf16[8,128]{1,0:T(8,128)(2,1)S(1)} %copy-done.10), channel_id=1, replica_groups=mesh['parts'=1,'head'=32] {'head'}, dimensions={0}, use_global_device_ids=true | all-gather | bytes 67584 | tf_op jit(solution)/shard_map/all_gather | solution.py:91
  512.9 14.9 %reshape.168 = f32[32,8,4,2048]{3,1,2,0:T(8,128)} reshape(f32[32,8,4,32,64]{4,3,1,2,0:T(8,128)} %bitcast.116) | data formatting | bytes 16777216 | tf_op jit(solution)/shard_map/convert_element_type | solution.py:97
  529.4 87.2 %reduce-scatter.3.cloned.1.call-done = f32[32,2048]{1,0:T(8,128)} async-done(((f32[1024,2048]{1,0:T(8,128)}), f32[32,2048]{1,0:T(8,128)}) %reduce-scatter.3.cloned.1.call-update) | async-done | bytes 262160 | tf_op jit(solution)/shard_map/reduce_scatter | solution.py:128
  623.0 114.5 %all-reduce.2.cloned.1.call-done = f32[8,2048]{1,0:T(8,128)} async-done(((f32[8,2048]{1,0:T(8,128)}), f32[8,2048]{1,0:T(8,128)}) %all-reduce.2.cloned.1.call-update) | async-done | bytes 65552 | tf_op jit(solution)/shard_map/psum | solution.py:135
  746.2 10.2 %mul.186 = f32[1024,2048]{1,0:T(8,128)} reshape(f32[32,8,4,2048]{3,2,1,0:T(4,128)} %mul.180) | data formatting | bytes 16777216 | tf_op jit(solution)/shard_map/mul | solution.py:141
  769.1 150.3 %reduce-scatter.5.cloned.1.call-done = f32[32,2048]{1,0:T(8,128)} async-done(((f32[1024,2048]{1,0:T(8,128)}), f32[32,2048]{1,0:T(8,128)}) %reduce-scatter.5.cloned.1.call-update) | async-done | bytes 262160 | tf_op jit(solution)/shard_map/reduce_scatter | solution.py:155
  (150 shorter events, 265.7 us)
Async XLA Ops:
  7.2 335.5 %copy-start = (bf16[256,4096]{1,0:T(8,128)(2,1)S(1)}, bf16[256,4096]{1,0:T(8,128)(2,1)}, u32[]{:S(2)}) copy-start(bf16[256,4096]{1,0:T(8,128)(2,1)} %param.23) | copy-start | bytes 6291460
  8.8 28.1 %all-to-all-start = ((bf16[32,2,256]{2,1,0:T(2,128)(2,1)}), bf16[32,2,256]{2,1,0:T(2,128)(2,1)S(1)}, u32[]{:S(2)}, u32[]{:S(2)}) async-start(bf16[32,2,256]{2,1,0:T(2,128)(2,1)} %reshape.176), calls=%async_computation | async-start | bytes 65536 | tf_op jit(solution)/shard_map/all_to_all | solution.py:72
  36.9 54.7 %all-to-all-start.1 = ((bf16[32,2,16384]{2,1,0:T(2,128)(2,1)}), bf16[32,2,16384]{2,1,0:T(2,128)(2,1)}, u32[]{:S(2)}, u32[]{:S(2)}) async-start(bf16[32,2,16384]{2,1,0:T(2,128)(2,1)} %reshape.178), calls=%async_computation.1 | async-start | bytes 4194304 | tf_op jit(solution)/shard_map/all_to_all | solution.py:69
  91.6 53.1 %all-to-all-start.2 = ((bf16[32,2,16384]{2,1,0:T(2,128)(2,1)}), bf16[32,2,16384]{2,1,0:T(2,128)(2,1)}, u32[]{:S(2)}, u32[]{:S(2)}) async-start(bf16[32,2,16384]{2,1,0:T(2,128)(2,1)} %reshape.180), calls=%async_computation.2 | async-start | bytes 4194304 | tf_op jit(solution)/shard_map/all_to_all | solution.py:70
  144.7 52.9 %all-to-all-start.3 = ((bf16[32,2,16384]{2,1,0:T(2,128)(2,1)}), bf16[32,2,16384]{2,1,0:T(2,128)(2,1)}, u32[]{:S(2)}, u32[]{:S(2)}) async-start(bf16[32,2,16384]{2,1,0:T(2,128)(2,1)} %reshape.182), calls=%async_computation.3 | async-start | bytes 4194304 | tf_op jit(solution)/shard_map/all_to_all | solution.py:71
  148.9 255.0 %all-gather.2.cloned.1.call-start = ((), (), s32[]{:S(2)}) async-start(), calls=%async_computation.6 | async-start | bytes 4325376 | tf_op jit(solution)/shard_map/all_gather | solution.py:90
  330.3 11.2 %copy-start.9 = (f32[8,128]{1,0:T(8,128)S(1)}, f32[8,128]{1,0:T(8,128)}, u32[]{:S(2)}) copy-start(f32[8,128]{1,0:T(8,128)} %get-tuple-element.86) | copy-start | bytes 12292
  330.3 12.3 %copy-start.12 = (s32[8]{0:T(128)S(1)}, s32[8]{0:T(128)}, u32[]{:S(2)}) copy-start(s32[8]{0:T(128)} %param.21) | copy-start | bytes 100
  342.5 274.2 %reduce-scatter.3.cloned.1.call-start = ((), (), s32[]{:S(2)}) async-start(), calls=%async_computation.7 | async-start | bytes 8650752 | tf_op jit(solution)/shard_map/reduce_scatter | solution.py:128
  434.0 14.8 %copy-start.8 = (f32[2048]{0:T(1024)S(1)}, f32[2048]{0:T(1024)}, u32[]{:S(2)}) copy-start(f32[2048]{0:T(1024)} %param.24) | copy-start | bytes 24580
  448.9 10.4 %copy-start.4 = (bf16[2048,256]{1,0:T(8,128)(2,1)S(1)}, bf16[2048,256]{1,0:T(8,128)(2,1)}, u32[]{:S(2)}) copy-start(bf16[2048,256]{1,0:T(8,128)(2,1)} %param.25) | copy-start | bytes 3145732
  448.9 11.7 %copy-start.6 = (bf16[2048,256]{1,0:T(8,128)(2,1)S(1)}, bf16[2048,256]{1,0:T(8,128)(2,1)}, u32[]{:S(2)}) copy-start(bf16[2048,256]{1,0:T(8,128)(2,1)} %param.26) | copy-start | bytes 3145732
  459.3 3.5 copy-start.3
  461.8 1.0 copy-start.1
  462.8 4.6 copy-start.11
  462.8 4.6 copy-start.10
  467.4 270.2 %all-reduce.2.cloned.1.call-start = ((), (), s32[]{:S(2)}) async-start(), calls=%async_computation.8 | async-start | bytes 131072 | tf_op jit(solution)/shard_map/psum | solution.py:135
  620.4 299.0 %reduce-scatter.5.cloned.1.call-start = ((), (), s32[]{:S(2)}) async-start(), calls=%async_computation.9 | async-start | bytes 8650752 | tf_op jit(solution)/shard_map/reduce_scatter | solution.py:155
  756.4 5.1 copy-start.2
  756.4 5.1 copy-start.5
  761.5 1.5 copy-start.7
Sparse Core Ops, SparseCore 0:
  342.6 61.2 all-gather.1
  467.5 149.1 reduce-scatter.2
  622.2 115.2 all-reduce.1
  767.8 151.5 reduce-scatter.4
where the time goes:
time: 940 us; the launch traced here: 929 us
  waiting for transfers between devices  458 us (49%)
  local copies, waits for them, and re-layouts  224 us (24%)
  matrix products  99.8 us (11%)
  other arithmetic  70.1 us (7%)
  blocking collectives  39.9 us (4%)
  starting transfers between devices  22.1 us (2%)
  between operations  14.4 us (2%)
    reduce_scatter x1, waiting for transfers between devices, body(): lax.psum_scatter(jnp.dot(gate_grad, gate_weight.T, preferred_element_type...  150 us
    psum x1, waiting for transfers between devices, body(): features = lax.psum(partial_value, 'head') / shower_counts[:, None]  114 us
    reduce_scatter x1, waiting for transfers between devices, body(): lax.psum_scatter(jnp.dot(hidden, down_weight, preferred_element_type=jnp....  87.2 us
    convert_element_type x4, local copies, waits for them, and re-layouts, body(): pooled_rows = pooled_all.reshape(showers, HEADS, devices, per_device, hea...  54.3 us
    unnamed x34, local copies, waits for them, and re-layouts  49.3 us
    dot_general x8, matrix products, attend_pair(): mixed = jnp.dot(weights, value_rows, preferred_element_type=jnp.float32)  48.2 us
    reduce_sum x8, other arithmetic, attend_pair(): jnp.sum(exponent, axis=1, keepdims=True)  40.4 us
    all_gather x1, blocking collectives, body(): lax.all_gather(window_count, 'head', axis=0, tiled=True)  39.9 us
  transfers between devices with their start and end apart: 8, of which 7 were waited for; matrix products, arithmetic and copies ran while one was open for 16% of the time, Pallas kernels for 0%

commit v1 on v0

--- a/solution.py
+++ b/solution.py
@@ -7,6 +7,11 @@
 HEADS = 32
 POOL = 16
 epsilon = 1e-06
+
+
+def gather_and_add(shard, mesh_axis):
+    parts = lax.all_gather(shard, mesh_axis)
+    return jnp.sum(parts, axis=0)
 
 
 def sinusoid(steps, embed_width):
@@ -132,7 +137,7 @@
         tiled=True,
     ).reshape(showers, per_device, model_width)
     partial_value = jnp.sum(own_count[:, :, None] * (own_pooled + own_mlp), axis=1)
-    features = lax.psum(partial_value, "head") / shower_counts[:, None]
+    features = gather_and_add(partial_value, "head") / shower_counts[:, None]
     logits = jnp.dot(features, class_matrix, precision=lax.Precision.HIGHEST) + class_bias
     exponent = jnp.exp(logits - jnp.max(logits, axis=1, keepdims=True))
     probability = exponent / jnp.sum(exponent, axis=1, keepdims=True)

time: 940 us -> 874 us (0.930)
  waiting for transfers between devices: 458 us -> 392 us
    psum x1 -> x0, waiting for transfers between devices: 114 us -> none  [body(): features = lax.psum(partial_value, 'head') / shower_counts[:, None]]
    all_gather x0 -> x1, waiting for transfers between devices: none -> 48.9 us  [gather_and_add(): parts = lax.all_gather(shard, mesh_axis)]
    unnamed x34 -> x36, local copies, waits for them, and re-layouts: 49.3 us -> 50.1 us
  transfers between devices with their start and end apart: 8 -> 8, of which waited for: 7 -> 7; matrix products, arithmetic and copies ran while one was open for 16% -> 17% of each run, Pallas kernels for 0% -> 0%
where the time goes in v1:
time: 874 us; the launch traced here: 862 us
  waiting for transfers between devices  392 us (45%)
  local copies, waits for them, and re-layouts  223 us (26%)
  matrix products  99.8 us (11%)
  other arithmetic  70.3 us (8%)
  blocking collectives  39.8 us (5%)
  starting transfers between devices  22.1 us (3%)
  between operations  14.4 us (2%)
    reduce_scatter x1, waiting for transfers between devices, body(): lax.psum_scatter(jnp.dot(gate_grad, gate_weight.T, preferred_element_type...  147 us
    reduce_scatter x1, waiting for transfers between devices, body(): lax.psum_scatter(jnp.dot(hidden, down_weight, preferred_element_type=jnp....  90.1 us
    convert_element_type x4, local copies, waits for them, and re-layouts, body(): pooled_rows = pooled_all.reshape(showers, HEADS, devices, per_device, hea...  54.3 us
    unnamed x36, local copies, waits for them, and re-layouts  50.1 us
    all_gather x1, waiting for transfers between devices, gather_and_add(): parts = lax.all_gather(shard, mesh_axis)  48.9 us
    dot_general x8, matrix products, attend_pair(): mixed = jnp.dot(weights, value_rows, preferred_element_type=jnp.float32)  48.2 us
    reduce_sum x8, other arithmetic, attend_pair(): jnp.sum(exponent, axis=1, keepdims=True)  40.4 us
    all_gather x1, blocking collectives, body(): lax.all_gather(window_count, 'head', axis=0, tiled=True)  39.8 us
  transfers between devices with their start and end apart: 8, of which 7 were waited for; matrix products, arithmetic and copies ran while one was open for 17% of the time, Pallas kernels for 0%

profile of v1, /device:TPU:0, one launch (start us, length us, event | category | flops | bytes accessed | tf_op | source)
XLA Modules:
  0.0 862.4 jit_solution(2568856933649873889)
XLA Ops:
  8.8 7.3 all-to-all-start
  29.0 7.9 reshape.179
  55.7 7.9 reshape.181
  63.6 28.0 %all-to-all-done.1 = bf16[32,2,16384]{2,1,0:T(2,128)(2,1)} async-done(((bf16[32,2,16384]{2,1,0:T(2,128)(2,1)}), bf16[32,2,16384]{2,1,0:T(2,128)(2,1)}, u32[]{:S(2)}, u32[]{:S(2)}) %all-to-all-start.1) | async-done | bytes 2097184 | tf_op jit(solution)/shard_map/all_to_all | solution.py:74
  108.8 7.9 reshape.183
  116.7 28.0 %all-to-all-done.2 = bf16[32,2,16384]{2,1,0:T(2,128)(2,1)} async-done(((bf16[32,2,16384]{2,1,0:T(2,128)(2,1)}), bf16[32,2,16384]{2,1,0:T(2,128)(2,1)}, u32[]{:S(2)}, u32[]{:S(2)}) %all-to-all-start.2) | async-done | bytes 2097184 | tf_op jit(solution)/shard_map/all_to_all | solution.py:75
  150.3 8.0 reshape.180
  163.8 7.9 reshape.182
  177.2 20.4 %all-to-all-done.3 = bf16[32,2,16384]{2,1,0:T(2,128)(2,1)} async-done(((bf16[32,2,16384]{2,1,0:T(2,128)(2,1)}), bf16[32,2,16384]{2,1,0:T(2,128)(2,1)}, u32[]{:S(2)}, u32[]{:S(2)}) %all-to-all-start.3) | async-done | bytes 2097184 | tf_op jit(solution)/shard_map/all_to_all | solution.py:76
  197.6 8.0 reshape.184
  211.1 119.2 %while.10 = (s32[]{:T(128)}, bf16[8,2048,64]{1,2,0:T(8,128)(2,1)}, pred[8,2048]{1,0:T(8,128)(4,1)S(1)}, bf16[8,2048,64]{2,1,0:T(8,128)(2,1)}, bf16[8,2048,64]{2,...) while((s32[]{:T(128)}, bf16[8,2048,64]{1,2,0:T(8,128)(2,1)}, pred[8,2048]{1,0:T(8,128)(4,1)S(1)}, ...), condition=%wide.region_3.4_spmd, body=%wide.region_0.3_spmd.sunk | while | flops 1124333568 | bytes 52238416 | solution.py:80
  348.4 10.4 %mul.175 = f32[1024,2048]{1,0:T(8,128)} reshape(f32[32,8,4,2048]{3,2,1,0:T(4,128)} %mul.174) | data formatting | bytes 16777216 | tf_op jit(solution)/shard_map/mul | solution.py:116
  364.2 10.0 %add.81 = f32[1024,2048]{1,0:T(8,128)} reshape(f32[32,8,4,2048]{3,2,1,0:T(4,128)} %add.80) | data formatting | bytes 16777216 | tf_op jit(solution)/shard_map/add | solution.py:116
  374.2 29.7 %all-gather.4.cloned.1.call-done = bf16[256,128,64]{1,2,0:T(8,128)(2,1)} async-done(((bf16[8,128,64]{1,2,0:T(8,128)(2,1)}), bf16[256,128,64]{1,2,0:T(8,128)(2,1)}) %all-gather.4.cloned.1.call-update) | async-done | bytes 4194320 | tf_op jit(solution)/shard_map/all_gather | solution.py:95
  409.5 12.8 %copy.161 = f32[256,128,64]{2,0,1:T(8,128)} copy(bf16[256,128,64]{1,2,0:T(8,128)(2,1)} %all-gather.4.cloned.1.call-done) | data formatting | bytes 12582912 | tf_op jit(solution)/shard_map/convert_element_type | solution.py:102
  422.2 11.9 %copy.163 = f32[32,8,4,32,64]{4,3,2,1,0:T(8,128)} copy(f32[32,8,4,32,64]{4,3,1,2,0:T(8,128)} %bitcast.117) | data formatting | bytes 16777216 | tf_op jit(solution)/shard_map/convert_element_type | solution.py:102
  434.1 14.8 %reshape.169 = f32[1024,2048]{1,0:T(8,128)} reshape(f32[32,8,4,32,64]{4,3,2,1,0:T(8,128)} %copy.163) | data formatting | bytes 16777216 | tf_op jit(solution)/shard_map/convert_element_type | solution.py:102
  448.9 10.4 %add_convert_fusion = bf16[1024,2048]{1,0:T(8,128)(2,1)S(1)} fusion(f32[1024,2048]{1,0:T(8,128)} %add.81, f32[1024,2048]{1,0:T(8,128)} %mul.175, f32[1024,2048]{1,0:T(8,128)} %reshape.169, f32[2048]{0:T(1024)S(1)} %copy-done.9, f32[1024]{0:T(1024)S(1)} %rsqrt.18), kind=kLoop, calls=%fused_computation.24 | loop fusion | flops 10485760 | bytes 29372416 | tf_op jit(solution)/shard_map/convert_element_type | solution.py:117
  467.5 39.8 %all_gather.12 = bf16[256,128]{1,0:T(8,128)(2,1)S(1)} all-gather(bf16[8,128]{1,0:T(8,128)(2,1)S(1)} %copy-done.11), channel_id=1, replica_groups=mesh['parts'=1,'head'=32] {'head'}, dimensions={0}, use_global_device_ids=true | all-gather | bytes 67584 | tf_op jit(solution)/shard_map/all_gather | solution.py:96
  510.1 14.9 %reshape.168 = f32[32,8,4,2048]{3,1,2,0:T(8,128)} reshape(f32[32,8,4,32,64]{4,3,1,2,0:T(8,128)} %bitcast.118) | data formatting | bytes 16777216 | tf_op jit(solution)/shard_map/convert_element_type | solution.py:102
  526.6 90.1 %reduce-scatter.3.cloned.1.call-done = f32[32,2048]{1,0:T(8,128)} async-done(((f32[1024,2048]{1,0:T(8,128)}), f32[32,2048]{1,0:T(8,128)}) %reduce-scatter.3.cloned.1.call-update) | async-done | bytes 262160 | tf_op jit(solution)/shard_map/reduce_scatter | solution.py:133
  623.7 48.9 %all-gather.6.cloned.1.call-done = f32[256,2048]{1,0:T(8,128)} async-done(((f32[8,2048]{1,0:T(8,128)}), f32[256,2048]{1,0:T(8,128)}) %all-gather.6.cloned.1.call-update) | async-done | bytes 2097168 | tf_op jit(solution)/shard_map/all_gather | solution.py:13
  683.1 10.2 %mul.186 = f32[1024,2048]{1,0:T(8,128)} reshape(f32[32,8,4,2048]{3,2,1,0:T(4,128)} %mul.180) | data formatting | bytes 16777216 | tf_op jit(solution)/shard_map/mul | solution.py:146
  706.0 147.3 %reduce-scatter.5.cloned.1.call-done = f32[32,2048]{1,0:T(8,128)} async-done(((f32[1024,2048]{1,0:T(8,128)}), f32[32,2048]{1,0:T(8,128)}) %reduce-scatter.5.cloned.1.call-update) | async-done | bytes 262160 | tf_op jit(solution)/shard_map/reduce_scatter | solution.py:160
  (153 shorter events, 265.4 us)
Async XLA Ops:
  7.2 335.5 %copy-start = (bf16[256,4096]{1,0:T(8,128)(2,1)S(1)}, bf16[256,4096]{1,0:T(8,128)(2,1)}, u32[]{:S(2)}) copy-start(bf16[256,4096]{1,0:T(8,128)(2,1)} %param.23) | copy-start | bytes 6291460
  8.8 28.1 %all-to-all-start = ((bf16[32,2,256]{2,1,0:T(2,128)(2,1)}), bf16[32,2,256]{2,1,0:T(2,128)(2,1)S(1)}, u32[]{:S(2)}, u32[]{:S(2)}) async-start(bf16[32,2,256]{2,1,0:T(2,128)(2,1)} %reshape.177), calls=%async_computation | async-start | bytes 65536 | tf_op jit(solution)/shard_map/all_to_all | solution.py:77
  36.9 54.7 %all-to-all-start.1 = ((bf16[32,2,16384]{2,1,0:T(2,128)(2,1)}), bf16[32,2,16384]{2,1,0:T(2,128)(2,1)}, u32[]{:S(2)}, u32[]{:S(2)}) async-start(bf16[32,2,16384]{2,1,0:T(2,128)(2,1)} %reshape.179), calls=%async_computation.1 | async-start | bytes 4194304 | tf_op jit(solution)/shard_map/all_to_all | solution.py:74
  91.6 53.1 %all-to-all-start.2 = ((bf16[32,2,16384]{2,1,0:T(2,128)(2,1)}), bf16[32,2,16384]{2,1,0:T(2,128)(2,1)}, u32[]{:S(2)}, u32[]{:S(2)}) async-start(bf16[32,2,16384]{2,1,0:T(2,128)(2,1)} %reshape.181), calls=%async_computation.2 | async-start | bytes 4194304 | tf_op jit(solution)/shard_map/all_to_all | solution.py:75
  144.7 52.9 %all-to-all-start.3 = ((bf16[32,2,16384]{2,1,0:T(2,128)(2,1)}), bf16[32,2,16384]{2,1,0:T(2,128)(2,1)}, u32[]{:S(2)}, u32[]{:S(2)}) async-start(bf16[32,2,16384]{2,1,0:T(2,128)(2,1)} %reshape.183), calls=%async_computation.3 | async-start | bytes 4194304 | tf_op jit(solution)/shard_map/all_to_all | solution.py:76
  148.9 255.0 %all-gather.4.cloned.1.call-start = ((), (), s32[]{:S(2)}) async-start(), calls=%async_computation.6 | async-start | bytes 4325376 | tf_op jit(solution)/shard_map/all_gather | solution.py:95
  330.3 11.2 %copy-start.10 = (f32[8,128]{1,0:T(8,128)S(1)}, f32[8,128]{1,0:T(8,128)}, u32[]{:S(2)}) copy-start(f32[8,128]{1,0:T(8,128)} %get-tuple-element.92) | copy-start | bytes 12292
  330.3 12.3 %copy-start.13 = (s32[8]{0:T(128)S(1)}, s32[8]{0:T(128)}, u32[]{:S(2)}) copy-start(s32[8]{0:T(128)} %param.21) | copy-start | bytes 100
  342.5 274.2 %reduce-scatter.3.cloned.1.call-start = ((), (), s32[]{:S(2)}) async-start(), calls=%async_computation.7 | async-start | bytes 8650752 | tf_op jit(solution)/shard_map/reduce_scatter | solution.py:133
  434.1 14.8 %copy-start.9 = (f32[2048]{0:T(1024)S(1)}, f32[2048]{0:T(1024)}, u32[]{:S(2)}) copy-start(f32[2048]{0:T(1024)} %param.24) | copy-start | bytes 24580
  448.9 10.4 %copy-start.5 = (bf16[2048,256]{1,0:T(8,128)(2,1)S(1)}, bf16[2048,256]{1,0:T(8,128)(2,1)}, u32[]{:S(2)}) copy-start(bf16[2048,256]{1,0:T(8,128)(2,1)} %param.25) | copy-start | bytes 3145732
  448.9 11.7 %copy-start.7 = (bf16[2048,256]{1,0:T(8,128)(2,1)S(1)}, bf16[2048,256]{1,0:T(8,128)(2,1)}, u32[]{:S(2)}) copy-start(bf16[2048,256]{1,0:T(8,128)(2,1)} %param.26) | copy-start | bytes 3145732
  459.3 3.5 copy-start.3
  461.9 1.0 copy-start.1
  462.9 4.6 copy-start.11
  467.4 205.2 %all-gather.6.cloned.1.call-start = ((), (), s32[]{:S(2)}) async-start(), calls=%async_computation.9 | async-start | bytes 2162688 | tf_op jit(solution)/shard_map/all_gather | solution.py:13
  509.1 0.8 copy-start.4
  510.1 110.4 %copy-start.12 = (s32[8]{0:T(128)S(1)}, s32[8]{0:T(128)}, u32[]{:S(2)}) copy-start(s32[8]{0:T(128)} %param.20) | copy-start | bytes 100
  620.4 232.9 %reduce-scatter.5.cloned.1.call-start = ((), (), s32[]{:S(2)}) async-start(), calls=%async_computation.8 | async-start | bytes 8650752 | tf_op jit(solution)/shard_map/reduce_scatter | solution.py:160
  693.2 5.1 copy-start.2
  693.2 5.1 copy-start.6
  698.3 1.5 copy-start.8
Sparse Core Ops, SparseCore 0:
  342.6 61.2 all-gather.3
  467.5 149.1 reduce-scatter.2
  620.5 52.0 all-gather.5
  704.6 148.6 reduce-scatter.4
